TPU v7x, 32 devices: a whole 2x2x4 slice. The times are simulated.
32 devices in a mesh: mem: 2 (over x), col: 16 (over z, y, core).
Axes of the slice: x: 2, y: 2, z: 4, core: 2. Of those that a mesh axis runs over, the one named last changes fastest.
Arguments:
- perturbations: bfloat16 [2, 16, 384, 768], P('mem', None, 'col'), may hold values from -6 to 6
- gradient: float32 [16, 384, 768], P(None, 'col'), may hold values from -6 to 6
- member_weights: float32 [2], P('mem'), may hold values from 0.5 to 2
- scale_weights: float32 [3], replicated, may hold values from 0.2 to 2
- lon_filter: bfloat16 [3, 768, 768], P(None, 'mem'), may hold values from -1 to 1.5
- lat_filter: bfloat16 [3, 384, 384], P(None, 'col'), may hold values from -1 to 1.5
Outputs:
- increment: float32 [16, 384, 768], P('mem', 'col')
All inputs are finite; a program needn't handle non-finite values.
Results may differ from a plain program's by a relative error of at most 0.01.
Values may be sent and summed in bfloat16 or wider, within the bound.
A program may use at most 64 MiB of HBM per device.

v0:
```python
import jax
import jax.numpy as jnp
from jax import lax
from jax.sharding import PartitionSpec as P


def on_device(perturbations, gradient, member_weights, scale_weights, lon_filter, lat_filter):
    member = perturbations[0].astype(jnp.float32)
    schur = (member * gradient).astype(jnp.bfloat16)
    levels = lax.all_to_all(schur, "col", split_axis=0, concat_axis=1, tiled=True)
    along = jnp.einsum(
        "laj,sij->lsai",
        levels,
        lax.all_gather(lon_filter, "mem", axis=1, tiled=True),
        preferred_element_type=jnp.float32,
    ).astype(jnp.bfloat16)
    across = jnp.einsum(
        "sab,lsbi->lsai",
        lax.all_gather(lat_filter, "col", axis=1, tiled=True),
        along,
        preferred_element_type=jnp.float32,
    )
    filtered = jnp.einsum("s,lsai->lai", scale_weights, across).astype(jnp.bfloat16)
    back = lax.all_to_all(filtered, "col", split_axis=1, concat_axis=0, tiled=True)
    terms = member_weights[0] * member * back.astype(jnp.float32)
    return lax.psum_scatter(terms, "mem", scatter_dimension=0, tiled=True)


def solution(mesh):
    placed = (
        P("mem", None, "col", None),
        P(None, "col", None),
        P("mem"),
        P(),
        P(None, "mem", None),
        P(None, "col", None),
    )
    return jax.shard_map(
        on_device, mesh=mesh, in_specs=placed, out_specs=P("mem", "col", None), check_vma=False
    )
```

profile of v0, /device:TPU:0, one launch (start us, length us, event | category | flops | bytes accessed | tf_op | source)
XLA Modules:
  0.0 129.6 jit_solution(12170853550535788724)
XLA Ops:
  6.5 0.0 copy-start
  6.5 0.0 copy-start.1
  6.5 0.0 copy-start.2
  6.5 0.0 all-gather.2.cloned.1.call-start
  6.5 0.7 all-gather.2.cloned.1.call-update
  7.3 0.4 copy-done.1
  7.6 0.4 copy-done.2
  8.0 0.0 copy-start.3
  8.0 0.9 fusion.5
  8.9 7.4 %all-to-all-start = ((bf16[16,24,768]{2,1,0:T(8,128)(2,1)}), bf16[16,24,768]{2,1,0:T(8,128)(2,1)S(1)}, u32[]{:S(2)}, u32[]{:S(2)}) async-start(bf16[16,24,768]{2,1,0:T(8,128)(2,1)} %fusion.5), calls=%async_computation | async-start | bytes 1179648 | tf_op jit(solution)/shard_map/all_to_all | solution.py:10
  16.4 0.0 copy-done.3
  16.4 29.1 %all_gather.7 = bf16[3,384,384]{2,1,0:T(8,128)(2,1)S(1)} all-gather(bf16[3,24,384]{2,1,0:T(8,128)(2,1)S(1)} %copy-done.3), channel_id=1, replica_groups=mesh['mem'=2,'col'=16] {'col'}, dimensions={1}, use_global_device_ids=true | all-gather | bytes 940032 | tf_op jit(solution)/shard_map/all_gather | solution.py:19
  45.5 0.0 all-to-all-done
  45.5 15.5 %all-gather.2.cloned.1.call-done = bf16[3,768,768]{2,1,0:T(8,128)(2,1)} async-done(((bf16[3,384,768]{2,1,0:T(8,128)(2,1)}), bf16[3,768,768]{2,1,0:T(8,128)(2,1)}) %all-gather.2.cloned.1.call-update) | async-done | bytes 3538960 | tf_op jit(solution)/shard_map/all_gather | solution.py:14
  61.0 5.9 %convolution_bitcast_fusion = bf16[3,384,768]{1,2,0:T(8,128)(2,1)} fusion(bf16[3,384,384]{2,1,0:T(8,128)(2,1)S(1)} %all_gather.7, bf16[384,768,1]{1,0,2:T(8,128)(2,1)S(1)} %bitcast.56, bf16[3,768,768]{2,1,0:T(8,128)(2,1)} %all-gather.2.cloned.1.call-done), kind=kOutput, calls=%fused_computation | convolution fusion | flops 2039316480 | bytes 6782976 | tf_op jit(solution)/shard_map/sab,lsbi->lsai/dot_general | solution.py:17
  66.9 4.0 %copy.12 = bf16[3,384,768]{2,0,1:T(4,128)(2,1)S(1)} copy(bf16[3,384,768]{1,2,0:T(8,128)(2,1)} %convolution_bitcast_fusion) | data formatting | bytes 3538944 | tf_op jit(solution)/shard_map/reshape.6
  70.9 0.0 copy-done
  70.9 1.4 %fusion.10 = bf16[1,384,768]{2,0,1:T(2,128)(2,1)S(1)} fusion(bf16[3,384,768]{2,0,1:T(4,128)(2,1)S(1)} %copy.12, f32[3]{0:T(128)S(1)} %copy-done), kind=kOutput, calls=%fused_computation.13 | convolution fusion | flops 1769472 | bytes 2359308 | tf_op jit(solution)/shard_map/s,lsai->lai/dot_general | solution.py:23
  72.2 0.1 copy.19
  72.3 0.9 copy.20
  73.2 0.5 broadcast
  73.8 4.4 %reduce = bf16[384,768]{1,0:T(8,128)(2,1)S(1)} reduce(bf16[384,1,768]{2,1,0:T(2,128)(2,1)S(1)} %bitcast.54, bf16[]{:T(256)} %broadcast), dimensions={1}, to_apply=%bitcast.51.reduce_sub_computation | reduce | bytes 1179650
  78.1 1.0 reshape.33
  79.1 5.6 %all-to-all-start.1 = ((bf16[16,2,9216]{2,1,0:T(2,128)(2,1)}), bf16[16,2,9216]{2,1,0:T(2,128)(2,1)S(1)}, u32[]{:S(2)}, u32[]{:S(2)}) async-start(bf16[16,2,9216]{2,1,0:T(2,128)(2,1)} %reshape.33), calls=%async_computation.1 | async-start | bytes 1179648 | tf_op jit(solution)/shard_map/all_to_all | solution.py:24
  84.7 0.0 reduce-scatter.2.cloned.1.call-start
  85.4 14.7 %all-to-all-done.1 = bf16[16,2,9216]{2,1,0:T(2,128)(2,1)S(1)} async-done(((bf16[16,2,9216]{2,1,0:T(2,128)(2,1)}), bf16[16,2,9216]{2,1,0:T(2,128)(2,1)S(1)}, u32[]{:S(2)}, u32[]{:S(2)}) %all-to-all-start.1) | async-done | bytes 589856 | tf_op jit(solution)/shard_map/all_to_all | solution.py:24
  100.1 0.5 reshape.34
  100.6 0.1 copy.14
  100.7 1.2 fusion.4
  101.8 0.0 reduce-scatter.2.cloned.1.call-update
  101.9 20.9 %reduce-scatter.2.cloned.1.call-done = f32[8,24,768]{2,1,0:T(8,128)} async-done(((f32[16,24,768]{2,1,0:T(8,128)}), f32[8,24,768]{2,1,0:T(8,128)}) %reduce-scatter.2.cloned.1.call-update) | async-done | bytes 589840 | tf_op jit(solution)/shard_map/reduce_scatter | solution.py:26
Async XLA Ops:
  6.5 64.3 %copy-start = (f32[3]{0:T(128)S(1)}, f32[3]{0:T(128)}, u32[]{:S(2)}) copy-start(f32[3]{0:T(128)} %param.9) | copy-start | bytes 40
  6.5 1.1 copy-start.1
  6.5 1.5 %copy-start.2 = (f32[16,24,768]{2,1,0:T(8,128)S(1)}, f32[16,24,768]{2,1,0:T(8,128)}, u32[]{:S(2)}) copy-start(f32[16,24,768]{2,1,0:T(8,128)} %param.7) | copy-start | bytes 3538948
  6.5 54.4 %all-gather.2.cloned.1.call-start = ((), (), s32[]{:S(2)}) async-start(), calls=%async_computation.3 | async-start | bytes 5308416 | tf_op jit(solution)/shard_map/all_gather | solution.py:14
  8.0 8.4 %copy-start.3 = (bf16[3,24,384]{2,1,0:T(8,128)(2,1)S(1)}, bf16[3,24,384]{2,1,0:T(8,128)(2,1)}, u32[]{:S(2)}) copy-start(bf16[3,24,384]{2,1,0:T(8,128)(2,1)} %param.11) | copy-start | bytes 165892
  8.9 36.5 %all-to-all-start = ((bf16[16,24,768]{2,1,0:T(8,128)(2,1)}), bf16[16,24,768]{2,1,0:T(8,128)(2,1)S(1)}, u32[]{:S(2)}, u32[]{:S(2)}) async-start(bf16[16,24,768]{2,1,0:T(8,128)(2,1)} %fusion.5), calls=%async_computation | async-start | bytes 1179648 | tf_op jit(solution)/shard_map/all_to_all | solution.py:10
  79.1 21.0 %all-to-all-start.1 = ((bf16[16,2,9216]{2,1,0:T(2,128)(2,1)}), bf16[16,2,9216]{2,1,0:T(2,128)(2,1)S(1)}, u32[]{:S(2)}, u32[]{:S(2)}) async-start(bf16[16,2,9216]{2,1,0:T(2,128)(2,1)} %reshape.33), calls=%async_computation.1 | async-start | bytes 1179648 | tf_op jit(solution)/shard_map/all_to_all | solution.py:24
  84.7 38.0 %reduce-scatter.2.cloned.1.call-start = ((), (), s32[]{:S(2)}) async-start(), calls=%async_computation.4 | async-start | bytes 1769472 | tf_op jit(solution)/shard_map/reduce_scatter | solution.py:26
Sparse Core Ops, SparseCore 0:
  8.9 52.0 all-gather.1
  102.0 20.7 reduce-scatter.1
where the time goes:
time: 130 us
  waiting for transfers between devices  51.8 us (40%)
  blocking collectives  29.1 us (22%)
  between operations  14.1 us (11%)
  starting transfers between devices  13.1 us (10%)
  local copies, waits for them, and re-layouts  7.76 us (6%)
  matrix products  7.27 us (6%)
  other arithmetic  6.47 us (5%)
    all_gather x1, blocking collectives, on_device(): lax.all_gather(lat_filter, 'col', axis=1, tiled=True)  29.1 us
    reduce_scatter x1, waiting for transfers between devices, on_device(): return lax.psum_scatter(terms, 'mem', scatter_dimension=0, tiled=True)  20.9 us
    all_gather x1, waiting for transfers between devices, on_device(): lax.all_gather(lon_filter, 'mem', axis=1, tiled=True)  15.5 us
    all_to_all x1, waiting for transfers between devices, on_device(): lax.all_to_all(filtered, 'col', split_axis=1, concat_axis=0, tiled=True)  14.7 us
    all_to_all x1, starting transfers between devices, on_device(): lax.all_to_all(schur, 'col', split_axis=0, concat_axis=1, tiled=True)  7.41 us
    dot_general x1, matrix products, on_device(): jnp.einsum('sab,lsbi->lsai', lax.all_gather(lat_filter, 'col', axis=1, ti...  5.91 us
    all_to_all x1, starting transfers between devices, on_device(): lax.all_to_all(filtered, 'col', split_axis=1, concat_axis=0, tiled=True)  5.62 us
    unnamed x1, other arithmetic  4.37 us
  transfers between devices with their start and end apart: 4, of which 3 were waited for; matrix products, arithmetic and copies ran while one was open for 1% of the time, Pallas kernels for 0%

commit v1 on v0

--- a/solution.py
+++ b/solution.py
@@ -4,15 +4,33 @@
 from jax.sharding import PartitionSpec as P
 
 
+def ring_apply(value, axis, dim, make, out_dim):
+    ways, here, hop = (lax.axis_size(axis), lax.axis_index(axis), value.shape[dim])
+    results = []
+    for far in range(ways):
+        arriving = (
+            lax.ppermute(value, axis, [(d, (d + 1) % ways) for d in range(ways)])
+            if far + 1 < ways
+            else value
+        )
+        results.append(make(value, (here - far) % ways * hop))
+        value = arriving
+    line = jnp.concatenate(results[::-1], axis=out_dim)
+    return jnp.roll(line, (here + 1) * results[0].shape[out_dim], axis=out_dim)
+
+
 def on_device(perturbations, gradient, member_weights, scale_weights, lon_filter, lat_filter):
     member = perturbations[0].astype(jnp.float32)
     schur = (member * gradient).astype(jnp.bfloat16)
     levels = lax.all_to_all(schur, "col", split_axis=0, concat_axis=1, tiled=True)
-    along = jnp.einsum(
-        "laj,sij->lsai",
-        levels,
-        lax.all_gather(lon_filter, "mem", axis=1, tiled=True),
-        preferred_element_type=jnp.float32,
+    along = ring_apply(
+        lon_filter,
+        "mem",
+        1,
+        lambda shard, offset: jnp.einsum(
+            "laj,sij->lsai", levels, shard, preferred_element_type=jnp.float32
+        ),
+        3,
     ).astype(jnp.bfloat16)
     across = jnp.einsum(
         "sab,lsbi->lsai",

time: 130 us -> 120 us (0.923)
  waiting for transfers between devices: 51.8 us -> 36.9 us
  matrix products: 7.27 us -> 9.75 us
  starting transfers between devices: 13.1 us -> 15.1 us
  other arithmetic: 6.47 us -> 7.86 us
    all_gather x1 -> x0, waiting for transfers between devices: 15.5 us -> none  [on_device(): lax.all_gather(lon_filter, 'mem', axis=1, tiled=True)]
    dot_general x0 -> x2, matrix products: none -> 3.69 us  [on_device(): jnp.einsum('laj,sij->lsai', levels, shard, preferred_element_type=jnp.flo...]
    ppermute x0 -> x1, starting transfers between devices: none -> 2.97 us  [ring_apply(): lax.ppermute(value, axis, [(d, (d + 1) % ways) for d in range(ways)])]
    all_to_all x1, starting transfers between devices: 7.41 us -> 5.94 us  [on_device(): lax.all_to_all(schur, 'col', split_axis=0, concat_axis=1, tiled=True)]
    convert_element_type x1, other arithmetic: 0.94 us -> 2.35 us  [on_device(): schur = (member * gradient).astype(jnp.bfloat16)]
  transfers between devices with their start and end apart: 4 -> 4, of which waited for: 3 -> 3; matrix products, arithmetic and copies ran while one was open for 1% -> 3% of each run, Pallas kernels for 0% -> 0%
where the time goes in v1:
time: 120 us
  waiting for transfers between devices  36.9 us (31%)
  blocking collectives  29.1 us (24%)
  starting transfers between devices  15.1 us (13%)
  between operations  14.2 us (12%)
  matrix products  9.75 us (8%)
  other arithmetic  7.86 us (7%)
  local copies, waits for them, and re-layouts  7.03 us (6%)
    all_gather x1, blocking collectives, on_device(): lax.all_gather(lat_filter, 'col', axis=1, tiled=True)  29.1 us
    reduce_scatter x1, waiting for transfers between devices, on_device(): return lax.psum_scatter(terms, 'mem', scatter_dimension=0, tiled=True)  21.8 us
    all_to_all x1, waiting for transfers between devices, on_device(): lax.all_to_all(filtered, 'col', split_axis=1, concat_axis=0, tiled=True)  14.7 us
    all_to_all x1, starting transfers between devices, on_device(): lax.all_to_all(filtered, 'col', split_axis=1, concat_axis=0, tiled=True)  6.16 us
    all_to_all x1, starting transfers between devices, on_device(): lax.all_to_all(schur, 'col', split_axis=0, concat_axis=1, tiled=True)  5.94 us
    dot_general x1, matrix products, on_device(): jnp.einsum('sab,lsbi->lsai', lax.all_gather(lat_filter, 'col', axis=1, ti...  4.7 us
    unnamed x1, other arithmetic  4.37 us
    another operation x1, local copies, waits for them, and re-layouts  3.98 us
  transfers between devices with their start and end apart: 4, of which 3 were waited for; matrix products, arithmetic and copies ran while one was open for 3% of the time, Pallas kernels for 0%

profile of v1, /device:TPU:0, one launch (start us, length us, event | category | flops | bytes accessed | tf_op | source)
XLA Modules:
  0.0 119.9 jit_solution(4190235565283901568)
XLA Ops:
  6.5 0.0 copy-start
  6.5 0.0 copy-start.3
  6.5 0.0 copy-start.2
  6.5 3.0 %collective-permute-start = (bf16[3,384,768]{2,1,0:T(8,128)(2,1)}, bf16[3,384,768]{2,1,0:T(8,128)(2,1)}, u32[]{:S(2)}, u32[]{:S(2)}) collective-permute-start(bf16[3,384,768]{2,1,0:T(8,128)(2,1)} %param.10), channel_id=1, source_target_pairs={{0,16},{16,0},{1,17},{17,1},{2,18},{18,2},{3,19},{19,3},{4,20},{20... | collective-permute-start | bytes 5308424 | tf_op jit(solution)/shard_map/ppermute | solution.py:12
  9.5 2.3 %fusion.7 = bf16[16,24,768]{2,1,0:T(8,128)(2,1)} fusion(f32[16,24,768]{2,1,0:T(8,128)} %param.7, bf16[1,16,24,768]{3,2,1,0:T(8,128)(2,1)} %param.6), kind=kLoop, calls=%fused_computation.15 | loop fusion | flops 884736 | bytes 2359296 | tf_op jit(solution)/shard_map/convert_element_type | solution.py:24
  11.9 5.9 %all-to-all-start = ((bf16[16,24,768]{2,1,0:T(8,128)(2,1)}), bf16[16,24,768]{2,1,0:T(8,128)(2,1)S(1)}, u32[]{:S(2)}, u32[]{:S(2)}) async-start(bf16[16,24,768]{2,1,0:T(8,128)(2,1)} %fusion.7), calls=%async_computation | async-start | bytes 1179648 | tf_op jit(solution)/shard_map/all_to_all | solution.py:25
  17.8 0.0 copy-done.2
  17.8 29.1 %all_gather.3 = bf16[3,384,384]{2,1,0:T(8,128)(2,1)S(1)} all-gather(bf16[3,24,384]{2,1,0:T(8,128)(2,1)S(1)} %copy-done.2), channel_id=1, replica_groups=mesh['mem'=2,'col'=16] {'col'}, dimensions={1}, use_global_device_ids=true | all-gather | bytes 940032 | tf_op jit(solution)/shard_map/all_gather | solution.py:37
  46.9 0.0 all-to-all-done
  46.9 0.0 copy-done.3
  46.9 1.1 convolution_bitcast_fusion.1
  48.0 0.4 collective-permute-done
  48.5 2.6 %convolution_bitcast_fusion.2 = bf16[1,3,384,384]{2,3,1,0:T(8,128)(2,1)S(1)} fusion(bf16[384,768,1]{1,0,2:T(8,128)(2,1)S(1)} %bitcast.65, bf16[3,384,768]{2,1,0:T(8,128)(2,1)} %collective-permute-done), kind=kOutput, calls=%fused_computation.11 | convolution fusion | flops 679477248 | bytes 3244032 | tf_op jit(solution)/shard_map/laj,sij->lsai/dot_general | solution.py:30
  51.0 4.7 %convolution_bitcast_fusion = bf16[3,384,768]{1,2,0:T(8,128)(2,1)} fusion(bf16[3,384,384]{2,1,0:T(8,128)(2,1)S(1)} %all_gather.3, s32[]{:T(128)S(6)} %select_n.14, bf16[1,3,384,384]{2,3,1,0:T(8,128)(2,1)S(1)} %convolution_bitcast_fusion.2, bf16[1,3,384,384]{2,3,1,0:T(8,128)(2,1)S(1)} %convolution_bitcast_fusion.1), kind=kOutput, calls=%fused_computation.8 | convolution fusion | flops 686555136 | bytes 4423684 | tf_op jit(solution)/shard_map/sab,lsbi->lsai/dot_general | solution.py:35
  55.7 4.0 %copy.8 = bf16[3,384,768]{2,0,1:T(4,128)(2,1)S(1)} copy(bf16[3,384,768]{1,2,0:T(8,128)(2,1)} %convolution_bitcast_fusion) | data formatting | bytes 3538944 | tf_op jit(solution)/shard_map/reshape.9
  59.7 0.0 copy-done
  59.7 1.4 %fusion.14 = bf16[1,384,768]{2,0,1:T(2,128)(2,1)S(1)} fusion(bf16[3,384,768]{2,0,1:T(4,128)(2,1)S(1)} %copy.8, f32[3]{0:T(128)S(1)} %copy-done), kind=kOutput, calls=%fused_computation.23 | convolution fusion | flops 1769472 | bytes 2359308 | tf_op jit(solution)/shard_map/s,lsai->lai/dot_general | solution.py:41
  61.1 0.1 copy.15
  61.2 0.9 copy.16
  62.1 0.5 broadcast
  62.6 4.4 %reduce = bf16[384,768]{1,0:T(8,128)(2,1)S(1)} reduce(bf16[384,1,768]{2,1,0:T(2,128)(2,1)S(1)} %bitcast.62, bf16[]{:T(256)} %broadcast), dimensions={1}, to_apply=%bitcast.59.reduce_sub_computation | reduce | bytes 1179650
  67.0 1.0 reshape.35
  68.0 6.2 %all-to-all-start.1 = ((bf16[16,2,9216]{2,1,0:T(2,128)(2,1)}), bf16[16,2,9216]{2,1,0:T(2,128)(2,1)S(1)}, u32[]{:S(2)}, u32[]{:S(2)}) async-start(bf16[16,2,9216]{2,1,0:T(2,128)(2,1)} %reshape.35), calls=%async_computation.1 | async-start | bytes 1179648 | tf_op jit(solution)/shard_map/all_to_all | solution.py:42
  74.1 0.0 reduce-scatter.2.cloned.1.call-start
  74.8 0.0 copy-start.1
  74.8 14.7 %all-to-all-done.1 = bf16[16,2,9216]{2,1,0:T(2,128)(2,1)S(1)} async-done(((bf16[16,2,9216]{2,1,0:T(2,128)(2,1)}), bf16[16,2,9216]{2,1,0:T(2,128)(2,1)S(1)}, u32[]{:S(2)}, u32[]{:S(2)}) %all-to-all-start.1) | async-done | bytes 589856 | tf_op jit(solution)/shard_map/all_to_all | solution.py:42
  89.5 0.5 reshape.36
  90.0 0.1 copy.10
  90.1 0.0 copy-done.1
  90.1 1.1 fusion.6
  91.2 0.0 reduce-scatter.2.cloned.1.call-update
  91.3 21.8 %reduce-scatter.2.cloned.1.call-done = f32[8,24,768]{2,1,0:T(8,128)} async-done(((f32[16,24,768]{2,1,0:T(8,128)}), f32[8,24,768]{2,1,0:T(8,128)}) %reduce-scatter.2.cloned.1.call-update) | async-done | bytes 589840 | tf_op jit(solution)/shard_map/reduce_scatter | solution.py:44
Async XLA Ops:
  6.5 53.2 %copy-start = (f32[3]{0:T(128)S(1)}, f32[3]{0:T(128)}, u32[]{:S(2)}) copy-start(f32[3]{0:T(128)} %param.9) | copy-start | bytes 40
  6.5 40.4 %copy-start.3 = (bf16[3,384,768]{2,1,0:T(8,128)(2,1)S(1)}, bf16[3,384,768]{2,1,0:T(8,128)(2,1)}, u32[]{:S(2)}) copy-start(bf16[3,384,768]{2,1,0:T(8,128)(2,1)} %param.10) | copy-start | bytes 5308420
  6.5 11.3 %copy-start.2 = (bf16[3,24,384]{2,1,0:T(8,128)(2,1)S(1)}, bf16[3,24,384]{2,1,0:T(8,128)(2,1)}, u32[]{:S(2)}) copy-start(bf16[3,24,384]{2,1,0:T(8,128)(2,1)} %param.11) | copy-start | bytes 165892
  6.5 41.9 %collective-permute-start = (bf16[3,384,768]{2,1,0:T(8,128)(2,1)}, bf16[3,384,768]{2,1,0:T(8,128)(2,1)}, u32[]{:S(2)}, u32[]{:S(2)}) collective-permute-start(bf16[3,384,768]{2,1,0:T(8,128)(2,1)} %param.10), channel_id=1, source_target_pairs={{0,16},{16,0},{1,17},{17,1},{2,18},{18,2},{3,19},{19,3},{4,20},{20... | collective-permute-start | bytes 5308424 | tf_op jit(solution)/shard_map/ppermute | solution.py:12
  11.9 35.1 %all-to-all-start = ((bf16[16,24,768]{2,1,0:T(8,128)(2,1)}), bf16[16,24,768]{2,1,0:T(8,128)(2,1)S(1)}, u32[]{:S(2)}, u32[]{:S(2)}) async-start(bf16[16,24,768]{2,1,0:T(8,128)(2,1)} %fusion.7), calls=%async_computation | async-start | bytes 1179648 | tf_op jit(solution)/shard_map/all_to_all | solution.py:25
  68.0 21.5 %all-to-all-start.1 = ((bf16[16,2,9216]{2,1,0:T(2,128)(2,1)}), bf16[16,2,9216]{2,1,0:T(2,128)(2,1)S(1)}, u32[]{:S(2)}, u32[]{:S(2)}) async-start(bf16[16,2,9216]{2,1,0:T(2,128)(2,1)} %reshape.35), calls=%async_computation.1 | async-start | bytes 1179648 | tf_op jit(solution)/shard_map/all_to_all | solution.py:42
  74.1 38.9 %reduce-scatter.2.cloned.1.call-start = ((), (), s32[]{:S(2)}) async-start(), calls=%async_computation.3 | async-start | bytes 1769472 | tf_op jit(solution)/shard_map/reduce_scatter | solution.py:44
  74.8 15.3 %copy-start.1 = (bf16[1,16,24,768]{3,2,1,0:T(8,128)(2,1)S(1)}, bf16[1,16,24,768]{3,2,1,0:T(8,128)(2,1)}, u32[]{:S(2)}) copy-start(bf16[1,16,24,768]{3,2,1,0:T(8,128)(2,1)} %param.6) | copy-start | bytes 1769476
Sparse Core Ops, SparseCore 0:
  91.4 21.6 reduce-scatter.1
